TPU v7x, 512 devices: a whole 4x4x16 slice. The times are simulated.
512 devices in a mesh: seq: 32 (over z, core), head: 16 (over x, y).
Axes of the slice: x: 4, y: 4, z: 16, core: 2. Of those that a mesh axis runs over, the one named last changes fastest.
Arguments:
- tokens: bfloat16 [8192, 4096], P('seq', 'head'), may hold values from -40 to 40
- norm_gain: float32 [4096], replicated, may hold values from 1.5 to 8
- w_qkv: bfloat16 [4096, 3, 2048], P(None, None, 'head'), may hold values from -0.09375 to 0.09375
- w_out: bfloat16 [2048, 4096], P('head'), may hold values from -0.75 to 0.75
- span_order: int32 [64], replicated, may hold values from 0 to 63, each once
- frame_id: int32 [8192], replicated, may hold values from 0 to 63, never falling along the last dimension, each value on 1 to 256 neighbouring positions
- camera_id: int32 [8192], replicated, may hold values from 0 to 5
Outputs:
- mixed: bfloat16 [8192, 4096], P('seq', 'head')
Inputs may be any that keep to these rules, and one draw needn't show every extreme that they name: `span_order`: each of the 64 spans appears once. `frame_id`: never falls along the sequence; every frame has 1 to 256 positions and one has exactly 256.
All inputs are finite; a program needn't handle non-finite values.
Results may differ from a plain program's by a relative error of at most 0.015.
The roundings to bfloat16 on the way count: a program that leaves them out, or rounds other values in their place, can miss the bound.
Values may be sent and summed in bfloat16 or wider, within the bound.
No kernel may reach another device: no remote copies, remote signals or barrier semaphores. Data moves between devices by JAX's collectives and lax.ppermute only.
A program may use at most 64 MiB of HBM per device.

v0:
```python
import jax
import jax.numpy as jnp
from jax import lax
from jax.sharding import PartitionSpec as P

D = 4096
HD = 128
epsilon = 1e-06
key_block = 1024


def stored_order(id_table, span_order):
    span_count = span_order.shape[0]
    return id_table.reshape(span_count, -1)[span_order].reshape(-1)


def visible_pairs(query_frames, query_cameras, key_frames, key_cameras):
    earlier = key_frames[None, :] < query_frames[:, None]
    same_view = (key_frames[None, :] == query_frames[:, None]) & (
        key_cameras[None, :] == query_cameras[:, None]
    )
    return earlier | same_view


def on_device(tokens, norm_gain, w_qkv, w_out, span_order, frame_id, camera_id):
    gathered = lax.all_gather(tokens, "head", axis=1, tiled=True)
    widened = gathered.astype(jnp.float32)
    inverse = lax.rsqrt(jnp.mean(widened * widened, axis=1, keepdims=True) + epsilon)
    normed = (widened * inverse * norm_gain).astype(jnp.bfloat16)
    row_count = tokens.shape[0]
    local_heads = w_out.shape[0] // HD
    projected = jnp.dot(
        normed, w_qkv.reshape(D, 3 * local_heads * HD), preferred_element_type=jnp.float32
    )
    projected = projected.astype(jnp.bfloat16).reshape(row_count, 3, local_heads, HD)
    queries = projected[:, 0]
    key_rows = projected[:, 1].reshape(row_count, local_heads * HD)
    value_rows = projected[:, 2].reshape(row_count, local_heads * HD)
    frames = stored_order(frame_id, span_order)
    cameras = stored_order(camera_id, span_order)
    first_row = lax.axis_index("seq") * row_count
    query_frames = lax.dynamic_slice_in_dim(frames, first_row, row_count, 0)
    query_cameras = lax.dynamic_slice_in_dim(cameras, first_row, row_count, 0)
    score_scale = HD ** (-0.5)

    def absorb(running, block_keys, block_values, key_start, frame_table, camera_table):
        key_count = block_keys.shape[0]
        key_frames = lax.dynamic_slice_in_dim(frame_table, key_start, key_count, 0)
        key_cameras = lax.dynamic_slice_in_dim(camera_table, key_start, key_count, 0)
        old_best, running_total, weighted = running
        scores = (
            jnp.einsum(
                "qhd,khd->hqk",
                queries,
                block_keys.reshape(key_count, local_heads, HD),
                preferred_element_type=jnp.float32,
            )
            * score_scale
        )
        allowed = visible_pairs(query_frames, query_cameras, key_frames, key_cameras)[None]
        block_best = jnp.max(jnp.where(allowed, scores, -jnp.inf), axis=2)
        new_best = jnp.maximum(old_best, block_best)
        weights = jnp.exp(jnp.where(allowed, scores - new_best[:, :, None], -jnp.inf))
        factor = jnp.exp(old_best - new_best)
        running_total = running_total * factor + jnp.sum(weights, axis=2)
        added = jnp.einsum(
            "hqk,khd->hqd",
            weights.astype(jnp.bfloat16),
            block_values.reshape(key_count, local_heads, HD),
            preferred_element_type=jnp.float32,
        )
        weighted = weighted * factor[:, :, None] + added
        return (new_best, running_total, weighted)

    initial = (
        jnp.full((local_heads, row_count), -1e30, jnp.float32),
        jnp.zeros((local_heads, row_count), jnp.float32),
        jnp.zeros((local_heads, row_count, HD), jnp.float32),
    )
    all_keys, all_values = (
        lax.all_gather(key_rows, "seq", axis=0, tiled=True),
        lax.all_gather(value_rows, "seq", axis=0, tiled=True),
    )
    running = initial
    length = all_keys.shape[0]
    block_rows = min(key_block, length)
    full_blocks = length // block_rows

    def advance(block_index, current):
        offset = block_index * block_rows
        block_keys = lax.dynamic_slice_in_dim(all_keys, offset, block_rows, 0)
        block_values = lax.dynamic_slice_in_dim(all_values, offset, block_rows, 0)
        return absorb(current, block_keys, block_values, 0 + offset, frames, cameras)

    running = lax.fori_loop(0, full_blocks, advance, running)
    attended = (running[2] / running[1][:, :, None]).astype(jnp.bfloat16)
    partial_value = jnp.einsum(
        "hqd,hde->qe",
        attended,
        w_out.reshape(local_heads, HD, D),
        preferred_element_type=jnp.float32,
    )
    mixed_rows = lax.psum_scatter(
        partial_value.astype(jnp.bfloat16), "head", scatter_dimension=1, tiled=True
    )
    return mixed_rows


def solution(mesh):
    placed = (P("seq", "head"), P(), P(None, None, "head"), P("head", None), P(), P(), P())
    return jax.shard_map(
        on_device, mesh=mesh, in_specs=placed, out_specs=P("seq", "head"), check_vma=False
    )
```

profile of v0, /device:TPU:2, one launch (start us, length us, event | category | flops | bytes accessed | tf_op | source)
XLA Modules:
  0.0 355.3 jit_solution(11500444099656653798)
XLA Ops:
  6.5 0.7 all-gather.6.cloned.1.call-update
  7.3 4.7 %copy.11 = bf16[4096,3,128]{0,2,1:T(8,128)(2,1)} copy(bf16[4096,3,128]{2,0,1:T(8,128)(2,1)} %param.11) | data formatting | bytes 6291456 | tf_op args[2]
  12.0 64.8 %all-gather.6.cloned.1.call-done = bf16[256,4096]{1,0:T(8,128)(2,1)} async-done(((bf16[256,256]{1,0:T(8,128)(2,1)}), bf16[256,4096]{1,0:T(8,128)(2,1)}) %all-gather.6.cloned.1.call-update) | async-done | bytes 2097168 | tf_op jit(solution)/shard_map/all_gather | solution.py:26
  76.8 2.2 fusion.16
  79.1 3.3 fusion.23
  83.3 0.7 all-gather.8.cloned.1.call-update
  85.6 70.4 %all-gather.10.cloned.1.call-done = bf16[8192,1,1,128]{0,3,1,2:T(8,128)(2,1)} async-done(((bf16[256,1,1,128]{0,3,1,2:T(8,128)(2,1)}), bf16[8192,1,1,128]{0,3,1,2:T(8,128)(2,1)}) %all-gather.10.cloned.1.call-update) | async-done | bytes 2097168 | tf_op jit(solution)/shard_map/all_gather | solution.py:82
  156.0 70.8 %all-gather.8.cloned.1.call-done = bf16[8192,1,1,128]{0,3,1,2:T(8,128)(2,1)} async-done(((bf16[256,1,1,128]{0,3,1,2:T(8,128)(2,1)}), bf16[8192,1,1,128]{0,3,1,2:T(8,128)(2,1)}) %all-gather.8.cloned.1.call-update) | async-done | bytes 2097168 | tf_op jit(solution)/shard_map/all_gather | solution.py:81
  226.8 33.6 %while.18 = (s32[]{:T(128)}, f32[1,256]{1,0:T(1,128)S(1)}, f32[1,256]{1,0:T(1,128)S(1)}, f32[1,256,128]{2,1,0:T(8,128)S(1)}, s32[8192]{0:T(1024)S(1)}, /*index=5...) while((s32[]{:T(128)}, f32[1,256]{1,0:T(1,128)S(1)}, ...), condition=%wide.region_4.5_spmd.clone, body=%wide.region_1.4_spmd.clone.sunk | while | flops 140608768 | bytes 4061407 | solution.py:95
  226.8 1.7 select_reduce_fusion.2
  229.3 1.7 fusion.41
  231.0 1.8 select_reduce_fusion.2
  233.5 1.7 fusion.41
  235.3 1.8 select_reduce_fusion.2
  237.0 0.7 fusion.39
  237.7 1.7 fusion.41
  239.5 1.8 select_reduce_fusion.2
  241.3 0.7 fusion.39
  242.0 1.7 fusion.41
  243.7 1.8 select_reduce_fusion.2
  245.5 0.7 fusion.39
  246.2 1.7 fusion.41
  247.9 1.8 select_reduce_fusion.2
  249.7 0.7 fusion.39
  250.4 1.7 fusion.41
  252.1 1.8 select_reduce_fusion.2
  253.9 0.7 fusion.39
  254.6 1.7 fusion.41
  256.3 1.8 select_reduce_fusion.2
  258.8 1.7 fusion.41
  260.5 2.1 convolution_convert_fusion
  262.6 86.2 %reduce-scatter.2.cloned.1.call-done = bf16[256,256]{1,0:T(8,128)(2,1)} async-done(((bf16[256,4096]{1,0:T(8,128)(2,1)}), bf16[256,256]{1,0:T(8,128)(2,1)}) %reduce-scatter.2.cloned.1.call-update) | async-done | bytes 131088 | tf_op jit(solution)/shard_map/reduce_scatter | solution.py:103
  (74 shorter events, 4.9 us)
Async XLA Ops:
  6.5 254.0 %copy-start = (bf16[128,4096]{1,0:T(8,128)(2,1)S(1)}, bf16[128,4096]{1,0:T(8,128)(2,1)}, u32[]{:S(2)}) copy-start(bf16[128,4096]{1,0:T(8,128)(2,1)} %param.12) | copy-start | bytes 3145732
  6.5 70.3 %all-gather.6.cloned.1.call-start = ((), (), s32[]{:S(2)}) async-start(), calls=%async_computation.1 | async-start | bytes 2228224 | tf_op jit(solution)/shard_map/all_gather | solution.py:26
  7.3 148.8 %all-gather.10.cloned.1.call-start = ((), (), s32[]{:S(2)}) async-start(), calls=%async_computation.4 | async-start | bytes 2162688 | tf_op jit(solution)/shard_map/all_gather | solution.py:82
  7.3 71.7 %copy-start.4 = (f32[4096]{0:T(1024)S(1)}, f32[4096]{0:T(1024)}, u32[]{:S(2)}) copy-start(f32[4096]{0:T(1024)} %param.10) | copy-start | bytes 49156
  76.8 2.3 copy-start.3
  79.1 5.0 %copy-start.5 = (s32[64]{0:T(128)S(1)}, s32[64]{0:T(128)}, u32[]{:S(2)}) copy-start(s32[64]{0:T(128)} %param.13) | copy-start | bytes 772
  79.1 5.0 %copy-start.1 = (s32[8192]{0:T(1024)S(1)}, s32[8192]{0:T(1024)}, u32[]{:S(2)}) copy-start(s32[8192]{0:T(1024)} %param.15) | copy-start | bytes 98308
  79.1 5.6 %copy-start.2 = (s32[8192]{0:T(1024)S(1)}, s32[8192]{0:T(1024)}, u32[]{:S(2)}) copy-start(s32[8192]{0:T(1024)} %param.14) | copy-start | bytes 98308
  83.3 143.6 %all-gather.8.cloned.1.call-start = ((), (), s32[]{:S(2)}) async-start(), calls=%async_computation.3 | async-start | bytes 2162688 | tf_op jit(solution)/shard_map/all_gather | solution.py:81
  84.0 264.8 %reduce-scatter.2.cloned.1.call-start = ((), (), s32[]{:S(2)}) async-start(), calls=%async_computation.2 | async-start | bytes 2228224 | tf_op jit(solution)/shard_map/reduce_scatter | solution.py:103
Sparse Core Ops, SparseCore 0:
  10.3 66.4 all-gather.5
  83.4 72.6 all-gather.9
  158.1 68.7 all-gather.7
  262.7 86.0 reduce-scatter.1
where the time goes:
time: 356 us; the launch traced here: 355 us
  waiting for transfers between devices  294 us (83%)
  matrix products  32.7 us (9%)
  between operations  13.3 us (4%)
  other arithmetic  7.89 us (2%)
  local copies, waits for them, and re-layouts  7.13 us (2%)
    reduce_scatter x1, waiting for transfers between devices, on_device(): lax.psum_scatter(partial_value.astype(jnp.bfloat16), 'head', scatter_dime...  86.2 us
    all_gather x1, waiting for transfers between devices, on_device(): lax.all_gather(key_rows, 'seq', axis=0, tiled=True)  70.8 us
    all_gather x1, waiting for transfers between devices, on_device(): lax.all_gather(value_rows, 'seq', axis=0, tiled=True)  70.4 us
    all_gather x1, waiting for transfers between devices, on_device(): gathered = lax.all_gather(tokens, 'head', axis=1, tiled=True)  64.8 us
    dot_general x8, matrix products, absorb(): jnp.einsum('qhd,khd->hqk', queries, block_keys.reshape(key_count, local_h...  14.1 us
    dot_general x8, matrix products, absorb(): jnp.einsum('hqk,khd->hqd', weights.astype(jnp.bfloat16), block_values.res...  13.2 us
  transfers between devices with their start and end apart: 4, of which 4 were waited for; matrix products, arithmetic and copies ran while one was open for 2% of the time, Pallas kernels for 0%

commit v1 on v0

--- a/solution.py
+++ b/solution.py
@@ -7,6 +7,11 @@
 HD = 128
 epsilon = 1e-06
 key_block = 1024
+
+
+def run_ranges_for(local_block, axis_name):
+    w_next = jnp.concatenate(jax.lax.all_gather(local_block, axis_name), 1)
+    return w_next
 
 
 def stored_order(id_table, span_order):
@@ -23,7 +28,7 @@
 
 
 def on_device(tokens, norm_gain, w_qkv, w_out, span_order, frame_id, camera_id):
-    gathered = lax.all_gather(tokens, "head", axis=1, tiled=True)
+    gathered = run_ranges_for(tokens, "head")
     widened = gathered.astype(jnp.float32)
     inverse = lax.rsqrt(jnp.mean(widened * widened, axis=1, keepdims=True) + epsilon)
     normed = (widened * inverse * norm_gain).astype(jnp.bfloat16)

time: 356 us -> 357 us (level)
  no operation moved by 1% of the time
where the time goes in v1:
time: 357 us
  waiting for transfers between devices  291 us (82%)
  matrix products  33.2 us (9%)
  between operations  13.2 us (4%)
  local copies, waits for them, and re-layouts  10.2 us (3%)
  other arithmetic  8.51 us (2%)
    reduce_scatter x1, waiting for transfers between devices, on_device(): lax.psum_scatter(partial_value.astype(jnp.bfloat16), 'head', scatter_dime...  86.3 us
    all_gather x1, waiting for transfers between devices, on_device(): lax.all_gather(key_rows, 'seq', axis=0, tiled=True)  70.8 us
    all_gather x1, waiting for transfers between devices, on_device(): lax.all_gather(value_rows, 'seq', axis=0, tiled=True)  70.4 us
    all_gather x1, waiting for transfers between devices, run_ranges_for(): w_next = jnp.concatenate(jax.lax.all_gather(local_block, axis_name), 1)  62 us
    dot_general x8, matrix products, absorb(): jnp.einsum('qhd,khd->hqk', queries, block_keys.reshape(key_count, local_h...  14.1 us
    dot_general x8, matrix products, absorb(): jnp.einsum('hqk,khd->hqd', weights.astype(jnp.bfloat16), block_values.res...  13.2 us
  transfers between devices with their start and end apart: 4, of which 4 were waited for; matrix products, arithmetic and copies ran while one was open for 2% of the time, Pallas kernels for 0%

profile of v1, /device:TPU:2, one launch (start us, length us, event | category | flops | bytes accessed | tf_op | source)
XLA Modules:
  0.0 356.8 jit_solution(1341115986836770903)
XLA Ops:
  6.5 0.7 all-gather.7.cloned.1.call-update
  7.3 0.7 mul.81
  8.0 4.7 %copy.17 = bf16[4096,3,128]{0,2,1:T(8,128)(2,1)} copy(bf16[4096,3,128]{2,0,1:T(8,128)(2,1)} %param.11) | data formatting | bytes 6291456 | tf_op args[2]
  12.7 62.0 %all-gather.7.cloned.1.call-done = bf16[4096,256]{1,0:T(8,128)(2,1)} async-done(((bf16[256,256]{1,0:T(8,128)(2,1)}), bf16[4096,256]{1,0:T(8,128)(2,1)}) %all-gather.7.cloned.1.call-update) | async-done | bytes 2097168 | tf_op jit(solution)/shard_map/all_gather | solution.py:13
  74.7 2.2 fusion.16
  77.6 2.4 copy.16
  80.0 3.8 %convolution_convert_fusion.1 = bf16[256,384]{1,0:T(8,128)(2,1)S(1)} fusion(bf16[256,4096]{0,1:T(8,128)(2,1)} %bitcast.53, bf16[4096,384]{0,1:T(8,128)(2,1)} %bitcast.50), kind=kOutput, calls=%fused_computation.33 | convolution fusion | flops 805404672 | bytes 5439488 | tf_op jit(solution)/shard_map/dot_general | solution.py:37
  84.7 0.7 all-gather.9.cloned.1.call-update
  87.0 70.4 %all-gather.11.cloned.1.call-done = bf16[8192,1,1,128]{0,3,1,2:T(8,128)(2,1)} async-done(((bf16[256,1,1,128]{0,3,1,2:T(8,128)(2,1)}), bf16[8192,1,1,128]{0,3,1,2:T(8,128)(2,1)}) %all-gather.11.cloned.1.call-update) | async-done | bytes 2097168 | tf_op jit(solution)/shard_map/all_gather | solution.py:87
  157.4 70.8 %all-gather.9.cloned.1.call-done = bf16[8192,1,1,128]{0,3,1,2:T(8,128)(2,1)} async-done(((bf16[256,1,1,128]{0,3,1,2:T(8,128)(2,1)}), bf16[8192,1,1,128]{0,3,1,2:T(8,128)(2,1)}) %all-gather.9.cloned.1.call-update) | async-done | bytes 2097168 | tf_op jit(solution)/shard_map/all_gather | solution.py:86
  228.2 33.6 %while.18 = (s32[]{:T(128)}, f32[1,256]{1,0:T(1,128)S(1)}, f32[1,256]{1,0:T(1,128)S(1)}, f32[1,256,128]{2,1,0:T(8,128)S(1)}, s32[8192]{0:T(1024)S(1)}, /*index=5...) while((s32[]{:T(128)}, f32[1,256]{1,0:T(1,128)S(1)}, ...), condition=%wide.region_4.5_spmd.clone, body=%wide.region_1.4_spmd.clone.sunk | while | flops 140608768 | bytes 4061407 | solution.py:100
  228.2 1.7 select_reduce_fusion.2
  230.0 0.7 fusion.34
  230.7 1.7 fusion.36
  232.4 1.8 select_reduce_fusion.2
  234.2 0.7 fusion.34
  234.9 1.7 fusion.36
  236.6 1.8 select_reduce_fusion.2
  238.4 0.7 fusion.34
  239.1 1.7 fusion.36
  240.9 1.8 select_reduce_fusion.2
  243.3 1.7 fusion.36
  245.1 1.8 select_reduce_fusion.2
  247.6 1.7 fusion.36
  249.3 1.8 select_reduce_fusion.2
  251.8 1.7 fusion.36
  253.5 1.8 select_reduce_fusion.2
  256.0 1.7 fusion.36
  257.7 1.8 select_reduce_fusion.2
  260.2 1.7 fusion.36
  261.9 2.1 convolution_convert_fusion
  264.0 86.3 %reduce-scatter.2.cloned.1.call-done = bf16[256,256]{1,0:T(8,128)(2,1)} async-done(((bf16[256,4096]{1,0:T(8,128)(2,1)}), bf16[256,256]{1,0:T(8,128)(2,1)}) %reduce-scatter.2.cloned.1.call-update) | async-done | bytes 131088 | tf_op jit(solution)/shard_map/reduce_scatter | solution.py:108
  (75 shorter events, 6.8 us)
Async XLA Ops:
  6.5 255.3 %copy-start = (bf16[128,4096]{1,0:T(8,128)(2,1)S(1)}, bf16[128,4096]{1,0:T(8,128)(2,1)}, u32[]{:S(2)}) copy-start(bf16[128,4096]{1,0:T(8,128)(2,1)} %param.12) | copy-start | bytes 3145732
  6.5 68.2 %all-gather.7.cloned.1.call-start = ((), (), s32[]{:S(2)}) async-start(), calls=%async_computation.2 | async-start | bytes 2228224 | tf_op jit(solution)/shard_map/all_gather | solution.py:13
  7.3 150.2 %all-gather.11.cloned.1.call-start = ((), (), s32[]{:S(2)}) async-start(), calls=%async_computation.4 | async-start | bytes 2162688 | tf_op jit(solution)/shard_map/all_gather | solution.py:87
  74.7 2.2 copy-start.1
  80.0 5.5 %copy-start.4 = (s32[64]{0:T(128)S(1)}, s32[64]{0:T(128)}, u32[]{:S(2)}) copy-start(s32[64]{0:T(128)} %param.13) | copy-start | bytes 772
  80.0 5.5 %copy-start.2 = (s32[8192]{0:T(1024)S(1)}, s32[8192]{0:T(1024)}, u32[]{:S(2)}) copy-start(s32[8192]{0:T(1024)} %param.15) | copy-start | bytes 98308
  80.0 6.1 %copy-start.3 = (s32[8192]{0:T(1024)S(1)}, s32[8192]{0:T(1024)}, u32[]{:S(2)}) copy-start(s32[8192]{0:T(1024)} %param.14) | copy-start | bytes 98308
  84.7 143.6 %all-gather.9.cloned.1.call-start = ((), (), s32[]{:S(2)}) async-start(), calls=%async_computation.3 | async-start | bytes 2162688 | tf_op jit(solution)/shard_map/all_gather | solution.py:86
  85.4 264.9 %reduce-scatter.2.cloned.1.call-start = ((), (), s32[]{:S(2)}) async-start(), calls=%async_computation.1 | async-start | bytes 2228224 | tf_op jit(solution)/shard_map/reduce_scatter | solution.py:108
Sparse Core Ops, SparseCore 0:
  10.3 64.3 all-gather.6
  84.8 72.5 all-gather.10
  159.5 68.7 all-gather.8
  264.1 86.1 reduce-scatter.1
